TPU v7x, 32 devices: a whole 2x2x4 slice. The times are simulated.
32 devices in a mesh: brick: 8 (over z, x), group: 4 (over y, core).
Axes of the slice: x: 2, y: 2, z: 4, core: 2. Of those that a mesh axis runs over, the one named last changes fastest.
Arguments:
- features: bfloat16 [32768, 96], P(('brick', 'group')), may hold values from -6 to 6
- order: int32 [32768], P(('brick', 'group')), may hold values from 0 to 1023, as said below
- face_list: int32 [8192], P(('brick', 'group')), may hold values from 0 to 1023, as said below
- face_count: int32 [64], P(('brick', 'group')), may hold values from 32 to 128, as said below
- kernel_map: int32 [27, 32768], P(None, ('brick', 'group')), may hold values from 0 to 1280, as said below
- weight: bfloat16 [27, 96, 256], replicated, may hold values from -0.15625 to 0.15625
- bias: float32 [256], replicated, may hold values from -3 to 3
- cotangent: bfloat16 [32768, 256], P(('brick', 'group')), may hold values from -6 to 6
Outputs:
- output: bfloat16 [32768, 256], P(('brick', 'group'))
- grad_in: bfloat16 [32768, 96], P(('brick', 'group'))
- weight_grad: float32 [27, 96, 256], replicated
Inputs may be any that keep to these rules, and one draw needn't show every extreme that they name: `order`: each device's 1024 entries are a permutation of 0 .. 1023. `face_list`: rows of the device's own brick. `face_count`: some list is full in every draw. `kernel_map`: the value 1024 + 2 * 128 names the zero row; offset 27 // 2 maps every voxel i to row i.
All inputs are finite; a program needn't handle non-finite values.
Results may differ from a plain program's by a relative error of at most 0.012.
Values may be sent and summed in bfloat16 or wider, within the bound.
No kernel may reach another device: no remote copies, remote signals or barrier semaphores. Data moves between devices by JAX's collectives and lax.ppermute only.
A program may use at most 64 MiB of HBM per device.

v0:
```python
import math
import jax
import jax.numpy as jnp
from jax import lax
from jax.sharding import PartitionSpec as P


def from_behind(array, axis, by):
    size = lax.axis_size(axis)
    pairs = [(i, i + by) for i in range(size) if 0 <= i + by < size]
    return lax.ppermute(array, axis, pairs)


def one_hot_rows(index, width):
    columns = jnp.arange(width, dtype=jnp.int32)
    return (index[:, None] == columns[None, :]).astype(jnp.bfloat16)


def pick_rows(selector, values):
    return jnp.dot(selector, values, preferred_element_type=jnp.float32).astype(jnp.bfloat16)


def spread_rows(selector, values):
    high_part = values.astype(jnp.bfloat16)
    low_part = (values - high_part.astype(jnp.float32)).astype(jnp.bfloat16)
    dims = (((0,), (0,)), ((), ()))
    first = lax.dot_general(selector, high_part, dims, preferred_element_type=jnp.float32)
    second = lax.dot_general(selector, low_part, dims, preferred_element_type=jnp.float32)
    return first + second


def on_device(features, order, face_list, face_count, kernel_map, weight, bias, cotangent):
    rows_here = features.shape[0]
    face_slots = face_list.shape[0] // 2
    order_pick = one_hot_rows(order, rows_here)
    sent_rows = pick_rows(order_pick, features)
    local_rows = lax.all_to_all(sent_rows, "brick", split_axis=0, concat_axis=0, tiled=True)
    slots = jnp.arange(face_slots, dtype=jnp.int32)
    lower_keep = (slots < face_count[0]).astype(jnp.bfloat16)[:, None]
    upper_keep = (slots < face_count[1]).astype(jnp.bfloat16)[:, None]
    lower_pick = one_hot_rows(face_list[:face_slots], rows_here) * lower_keep
    upper_pick = one_hot_rows(face_list[face_slots:], rows_here) * upper_keep
    lower_rows = pick_rows(lower_pick, local_rows)
    upper_rows = pick_rows(upper_pick, local_rows)
    prev_upper = from_behind(upper_rows, "brick", 1)
    next_lower = from_behind(lower_rows, "brick", -1)
    zero_row = jnp.zeros((1, local_rows.shape[1]), jnp.bfloat16)
    extended = jnp.concatenate([local_rows, prev_upper, next_lower, zero_row], 0)
    ext_count = extended.shape[0]

    def forward(summed, operands):
        map_row, kernel = operands
        gathered = pick_rows(one_hot_rows(map_row, ext_count), extended)
        return (summed + jnp.dot(gathered, kernel, preferred_element_type=jnp.float32), None)

    start = jnp.zeros((rows_here, weight.shape[2]), jnp.float32)
    pre, _ = lax.scan(forward, start, (kernel_map, weight))
    pre = pre + bias
    output = jnp.maximum(pre, 0.0).astype(jnp.bfloat16)
    pre_grad = jnp.where(pre > 0, cotangent, jnp.zeros_like(cotangent))

    def offset_grads(ext_grad, map_row, kernel):
        selector = one_hot_rows(map_row, ext_count)
        gathered = pick_rows(selector, extended)
        kernel_grad = lax.dot_general(
            gathered, pre_grad, (((0,), (0,)), ((), ())), preferred_element_type=jnp.float32
        )
        contrib = lax.dot_general(
            pre_grad, kernel, (((1,), (1,)), ((), ())), preferred_element_type=jnp.float32
        )
        return (ext_grad + spread_rows(selector, contrib), kernel_grad)

    zeros_grad = jnp.zeros((ext_count, extended.shape[1]), jnp.float32)

    def backward(ext_grad, operands):
        map_row, kernel = operands
        return offset_grads(ext_grad, map_row, kernel)

    ext_grad, kernel_grads = lax.scan(backward, zeros_grad, (kernel_map, weight))
    weight_sum = lax.psum(kernel_grads, ("brick", "group"))
    to_prev = ext_grad[rows_here : rows_here + face_slots]
    to_next = ext_grad[rows_here + face_slots : rows_here + 2 * face_slots]
    from_prev = from_behind(to_next.astype(jnp.bfloat16), "brick", 1).astype(to_next.dtype)
    from_next = from_behind(to_prev.astype(jnp.bfloat16), "brick", -1).astype(to_prev.dtype)
    local_grad = (
        ext_grad[:rows_here]
        + spread_rows(lower_pick, from_prev)
        + spread_rows(upper_pick, from_next)
    )
    brick_grad = local_grad.astype(jnp.bfloat16)
    returned = lax.all_to_all(brick_grad, "brick", split_axis=0, concat_axis=0, tiled=True)
    grad_in = lax.dot_general(
        order_pick, returned, (((0,), (0,)), ((), ())), preferred_element_type=jnp.float32
    ).astype(jnp.bfloat16)
    voxel_total = lax.axis_size("brick") * lax.axis_size("group") * rows_here
    weight_grad = weight_sum * jnp.float32(1.0 / math.sqrt(voxel_total))
    return (output, grad_in, weight_grad)


def solution(mesh):
    return jax.shard_map(
        on_device,
        mesh=mesh,
        in_specs=(
            P(("brick", "group"), None),
            P(("brick", "group")),
            P(("brick", "group")),
            P(("brick", "group")),
            P(None, ("brick", "group")),
            P(),
            P(),
            P(("brick", "group"), None),
        ),
        out_specs=(P(("brick", "group"), None), P(("brick", "group"), None), P()),
        check_vma=False,
    )
```

profile of v0, /device:TPU:0, one launch (start us, length us, event | category | flops | bytes accessed | tf_op | source)
XLA Modules:
  0.0 454.1 jit_solution(2190139345262719592)
XLA Ops:
  10.5 7.2 %all-to-all-start = ((bf16[8,128,96]{1,2,0:T(8,128)(2,1)}), bf16[8,128,96]{1,2,0:T(8,128)(2,1)S(1)}, u32[]{:S(2)}, u32[]{:S(2)}) async-start(bf16[8,128,96]{1,2,0:T(8,128)(2,1)} %bitcast.53), calls=%async_computation | async-start | bytes 393216 | tf_op jit(solution)/shard_map/all_to_all | solution.py:37
  21.3 4.4 all-to-all-done
  26.0 3.0 collective-permute-start
  30.6 4.4 collective-permute-done.1
  35.3 92.4 %while.24 = (s32[]{:T(128)}, f32[1024,256]{1,0:T(8,128)S(1)}, s32[27,1024]{1,0:T(8,128)}, bf16[1281,96]{1,0:T(8,128)(2,1)S(1)}, bf16[27,96,256]{2,1,0:T(8,128)(2,1)}, /*index=5*/s32[]{:T(128)}, s32[]{:T(128)}) while((s32[]{:T(128)}, f32[1024,256]{1,0:T(8,128)S(1)}, s32[27,1024]{1,0:T(8,128)}, bf16[1281,96]{1,0:T(8,128)(2,1)S(1)}, ...), condition=%wide.region_1.2_spmd.clone, body=%wide.region_0.1_spmd.clone.sunk | while | flops 304120832 | bytes 2404647 | solution.py:57
  36.2 2.6 convolution_add_fusion.4
  39.6 2.6 convolution_add_fusion.4
  43.0 2.6 convolution_add_fusion.4
  46.4 2.6 convolution_add_fusion.4
  49.8 2.6 convolution_add_fusion.4
  53.3 2.6 convolution_add_fusion.4
  56.7 2.6 convolution_add_fusion.4
  60.1 2.6 convolution_add_fusion.4
  63.5 2.6 convolution_add_fusion.4
  66.9 2.6 convolution_add_fusion.4
  70.4 2.6 convolution_add_fusion.4
  73.8 2.6 convolution_add_fusion.4
  77.2 2.6 convolution_add_fusion.4
  80.6 2.6 convolution_add_fusion.4
  84.0 2.6 convolution_add_fusion.4
  87.5 2.6 convolution_add_fusion.4
  90.9 2.6 convolution_add_fusion.4
  94.3 2.6 convolution_add_fusion.4
  97.7 2.6 convolution_add_fusion.4
  101.1 2.6 convolution_add_fusion.4
  104.5 2.6 convolution_add_fusion.4
  108.0 2.6 convolution_add_fusion.4
  111.4 2.6 convolution_add_fusion.4
  114.8 2.6 convolution_add_fusion.4
  118.2 2.6 convolution_add_fusion.4
  121.6 2.6 convolution_add_fusion.4
  125.1 2.6 convolution_add_fusion.4
  127.9 176.2 %while.25 = (s32[]{:T(128)}, f32[1281,96]{0,1:T(8,128)S(1)}, f32[27,96,256]{2,1,0:T(8,128)}, s32[27,1024]{1,0:T(8,128)}, bf16[27,96,256]{2,1,0:T(8,128)(2,1)}, /...) while((s32[]{:T(128)}, f32[1281,96]{0,1:T(8,128)S(1)}, ...), condition=%wide.region_3.4_spmd.clone, body=%wide.region_2.3_spmd.clone.sunk | while | flops 861121792 | bytes 4609851 | solution.py:79
  132.3 2.1 fusion.103
  138.9 2.1 fusion.103
  145.4 2.1 fusion.103
  151.9 2.1 fusion.103
  158.4 2.1 fusion.103
  165.0 2.1 fusion.103
  171.5 2.1 fusion.103
  178.0 2.1 fusion.103
  191.1 2.1 fusion.103
  197.6 2.1 fusion.103
  305.5 4.5 %collective-permute-start.2 = (bf16[128,96]{0,1:T(8,128)(2,1)S(1)}, bf16[128,96]{0,1:T(8,128)(2,1)S(1)}, u32[]{:S(2)}, u32[]{:S(2)}) collective-permute-start(bf16[128,96]{0,1:T(8,128)(2,1)S(1)} %get-tuple-element.149), channel_id=1, source_target_pairs={{0,4},{4,8},{8,12},{12,16},{16,20},{20,24},{24,28},{1,5},{5,9},{9,... | collective-permute-start | bytes 73736 | tf_op jit(solution)/shard_map/ppermute | solution.py:11
  313.2 6.1 %all-to-all-start.1 = ((bf16[8,128,96]{1,2,0:T(8,128)(2,1)}), bf16[8,128,96]{1,2,0:T(8,128)(2,1)S(1)}, u32[]{:S(2)}, u32[]{:S(2)}) async-start(bf16[8,128,96]{1,2,0:T(8,128)(2,1)} %bitcast.52), calls=%async_computation.1 | async-start | bytes 393216 | tf_op jit(solution)/shard_map/all_to_all | solution.py:91
  320.1 8.6 %all-to-all-done.1 = bf16[8,128,96]{1,2,0:T(8,128)(2,1)S(1)} async-done(((bf16[8,128,96]{1,2,0:T(8,128)(2,1)}), bf16[8,128,96]{1,2,0:T(8,128)(2,1)S(1)}, u32[]{:S(2)}, u32[]{:S(2)}) %all-to-all-start.1) | async-done | bytes 196640 | tf_op jit(solution)/shard_map/all_to_all | solution.py:91
  330.3 113.4 %all-reduce.2.cloned.1.call-done = f32[27,96,256]{2,1,0:T(8,128)} async-done(((f32[27,96,256]{2,1,0:T(8,128)}), f32[27,96,256]{2,1,0:T(8,128)}) %all-reduce.2.cloned.1.call-update) | async-done | bytes 2654224 | tf_op jit(solution)/shard_map/psum | solution.py:80
  443.7 3.6 broadcast_multiply_fusion
  (192 shorter events, 191.4 us)
Async XLA Ops:
  7.2 0.9 copy-start
  10.5 15.2 %all-to-all-start = ((bf16[8,128,96]{1,2,0:T(8,128)(2,1)}), bf16[8,128,96]{1,2,0:T(8,128)(2,1)S(1)}, u32[]{:S(2)}, u32[]{:S(2)}) async-start(bf16[8,128,96]{1,2,0:T(8,128)(2,1)} %bitcast.53), calls=%async_computation | async-start | bytes 393216 | tf_op jit(solution)/shard_map/all_to_all | solution.py:37
  17.8 425.9 %all-reduce.2.cloned.1.call-start = ((), (), s32[]{:S(2)}) async-start(), calls=%async_computation.2 | async-start | bytes 5308416 | tf_op jit(solution)/shard_map/psum | solution.py:80
  26.0 4.6 %collective-permute-start = (bf16[128,96]{0,1:T(8,128)(2,1)S(1)}, bf16[128,96]{0,1:T(8,128)(2,1)S(1)}, u32[]{:S(2)}, u32[]{:S(2)}) collective-permute-start(bf16[128,96]{0,1:T(8,128)(2,1)S(1)} %convolution_convert_fusion.1), channel_id=1, source_target_pairs={{0,4},{4,8},{8,12},{12,16},{16,20},{20,24},{24,28},{1,5},{5,9},{9,... | collective-permute-start | bytes 73736 | tf_op jit(solution)/shard_map/ppermute | solution.py:11
  29.3 5.7 %collective-permute-start.1 = (bf16[128,96]{0,1:T(8,128)(2,1)S(1)}, bf16[128,96]{0,1:T(8,128)(2,1)S(1)}, u32[]{:S(2)}, u32[]{:S(2)}) collective-permute-start(bf16[128,96]{0,1:T(8,128)(2,1)S(1)} %convolution_convert_fusion), channel_id=1, source_target_pairs={{4,0},{8,4},{12,8},{16,12},{20,16},{24,20},{28,24},{5,1},{9,5},{13... | collective-permute-start | bytes 73736 | tf_op jit(solution)/shard_map/ppermute | solution.py:11
  35.3 92.4 %copy-start.1 = (bf16[1024,256]{1,0:T(8,128)(2,1)S(1)}, bf16[1024,256]{1,0:T(8,128)(2,1)}, u32[]{:S(2)}) copy-start(bf16[1024,256]{1,0:T(8,128)(2,1)} %param.19) | copy-start | bytes 1572868
  35.3 92.4 %copy-start.2 = (f32[256]{0:T(256)S(1)}, f32[256]{0:T(256)}, u32[]{:S(2)}) copy-start(f32[256]{0:T(256)} %param.18) | copy-start | bytes 3076
  304.2 5.9 %collective-permute-start.3 = (bf16[128,96]{0,1:T(8,128)(2,1)S(1)}, bf16[128,96]{0,1:T(8,128)(2,1)S(1)}, u32[]{:S(2)}, u32[]{:S(2)}) collective-permute-start(bf16[128,96]{0,1:T(8,128)(2,1)S(1)} %get-tuple-element.150), channel_id=1, source_target_pairs={{4,0},{8,4},{12,8},{16,12},{20,16},{24,20},{28,24},{5,1},{9,5},{13... | collective-permute-start | bytes 73736 | tf_op jit(solution)/shard_map/ppermute | solution.py:11
  305.5 6.1 %collective-permute-start.2 = (bf16[128,96]{0,1:T(8,128)(2,1)S(1)}, bf16[128,96]{0,1:T(8,128)(2,1)S(1)}, u32[]{:S(2)}, u32[]{:S(2)}) collective-permute-start(bf16[128,96]{0,1:T(8,128)(2,1)S(1)} %get-tuple-element.149), channel_id=1, source_target_pairs={{0,4},{4,8},{8,12},{12,16},{16,20},{20,24},{24,28},{1,5},{5,9},{9,... | collective-permute-start | bytes 73736 | tf_op jit(solution)/shard_map/ppermute | solution.py:11
  310.4 18.4 %copy-start.3 = (s32[1024]{0:T(1024)S(1)}, s32[1024]{0:T(1024)}, u32[]{:S(2)}) copy-start(s32[1024]{0:T(1024)} %param.13) | copy-start | bytes 12292
  313.2 15.6 %all-to-all-start.1 = ((bf16[8,128,96]{1,2,0:T(8,128)(2,1)}), bf16[8,128,96]{1,2,0:T(8,128)(2,1)S(1)}, u32[]{:S(2)}, u32[]{:S(2)}) async-start(bf16[8,128,96]{1,2,0:T(8,128)(2,1)} %bitcast.52), calls=%async_computation.1 | async-start | bytes 393216 | tf_op jit(solution)/shard_map/all_to_all | solution.py:91
Sparse Core Ops, SparseCore 0:
  305.6 138.0 all-reduce.1
where the time goes:
time: 461 us; the launch traced here: 454 us
  matrix products  231 us (50%)
  waiting for transfers between devices  132 us (29%)
  local copies, waits for them, and re-layouts  46.2 us (10%)
  starting transfers between devices  23.5 us (5%)
  between operations  14.3 us (3%)
  other arithmetic  6.1 us (1%)
    psum x1, waiting for transfers between devices, on_device(): weight_sum = lax.psum(kernel_grads, ('brick', 'group'))  113 us
    dot_general x27, matrix products, forward(): jnp.dot(gathered, kernel, preferred_element_type=jnp.float32)  70.8 us
    dot_general x27, matrix products, offset_grads(): lax.dot_general(gathered, pre_grad, (((0,), (0,)), ((), ())), preferred_e...  57.3 us
    dynamic_slice x54, local copies, waits for them, and re-layouts, on_device(): pre, _ = lax.scan(forward, start, (kernel_map, weight))  41.5 us
    dot_general x29, matrix products, spread_rows(): lax.dot_general(selector, high_part, dims, preferred_element_type=jnp.flo...  35.7 us
    dot_general x29, matrix products, spread_rows(): lax.dot_general(selector, low_part, dims, preferred_element_type=jnp.floa...  34.1 us
    dot_general x27, matrix products, offset_grads(): lax.dot_general(pre_grad, kernel, (((1,), (1,)), ((), ())), preferred_ele...  29.2 us
    ppermute x4, starting transfers between devices, from_behind(): return lax.ppermute(array, axis, pairs)  10.1 us
  transfers between devices with their start and end apart: 7, of which 5 were waited for; matrix products, arithmetic and copies ran while one was open for 2% of the time, Pallas kernels for 0%

commit v1 on v0

--- a/solution.py
+++ b/solution.py
@@ -77,7 +77,8 @@
         return offset_grads(ext_grad, map_row, kernel)
 
     ext_grad, kernel_grads = lax.scan(backward, zeros_grad, (kernel_map, weight))
-    weight_sum = lax.psum(kernel_grads, ("brick", "group"))
+    half = lax.psum(kernel_grads, "group")
+    weight_sum = lax.psum(half, "brick")
     to_prev = ext_grad[rows_here : rows_here + face_slots]
     to_next = ext_grad[rows_here + face_slots : rows_here + 2 * face_slots]
     from_prev = from_behind(to_next.astype(jnp.bfloat16), "brick", 1).astype(to_next.dtype)

time: 461 us -> 505 us (1.095)
  waiting for transfers between devices: 132 us -> 175 us
    psum x1 -> x2, waiting for transfers between devices: 113 us -> 152 us  [the longest x1 92.5 us: on_device(): weight_sum = lax.psum(half, 'brick')]
  transfers between devices with their start and end apart: 7 -> 8, of which waited for: 5 -> 6; matrix products, arithmetic and copies ran while one was open for 2% -> 2% of each run, Pallas kernels for 0% -> 0%
where the time goes in v1:
time: 505 us; the launch traced here: 498 us
  matrix products  231 us (46%)
  waiting for transfers between devices  175 us (35%)
  local copies, waits for them, and re-layouts  46.2 us (9%)
  starting transfers between devices  24.7 us (5%)
  between operations  14.3 us (3%)
  other arithmetic  6.1 us (1%)
    psum x1, waiting for transfers between devices, on_device(): weight_sum = lax.psum(half, 'brick')  92.5 us
    dot_general x27, matrix products, forward(): jnp.dot(gathered, kernel, preferred_element_type=jnp.float32)  70.8 us
    psum x1, waiting for transfers between devices, on_device(): half = lax.psum(kernel_grads, 'group')  59.4 us
    dot_general x27, matrix products, offset_grads(): lax.dot_general(gathered, pre_grad, (((0,), (0,)), ((), ())), preferred_e...  57.3 us
    dynamic_slice x54, local copies, waits for them, and re-layouts, on_device(): pre, _ = lax.scan(forward, start, (kernel_map, weight))  41.5 us
    dot_general x29, matrix products, spread_rows(): lax.dot_general(selector, high_part, dims, preferred_element_type=jnp.flo...  35.7 us
    dot_general x29, matrix products, spread_rows(): lax.dot_general(selector, low_part, dims, preferred_element_type=jnp.floa...  34.1 us
    dot_general x27, matrix products, offset_grads(): lax.dot_general(pre_grad, kernel, (((1,), (1,)), ((), ())), preferred_ele...  29.2 us
  transfers between devices with their start and end apart: 8, of which 6 were waited for; matrix products, arithmetic and copies ran while one was open for 2% of the time, Pallas kernels for 0%

profile of v1, /device:TPU:0, one launch (start us, length us, event | category | flops | bytes accessed | tf_op | source)
XLA Modules:
  0.0 498.1 jit_solution(8192842222040322379)
XLA Ops:
  10.5 7.2 %all-to-all-start = ((bf16[8,128,96]{1,2,0:T(8,128)(2,1)}), bf16[8,128,96]{1,2,0:T(8,128)(2,1)S(1)}, u32[]{:S(2)}, u32[]{:S(2)}) async-start(bf16[8,128,96]{1,2,0:T(8,128)(2,1)} %bitcast.53), calls=%async_computation | async-start | bytes 393216 | tf_op jit(solution)/shard_map/all_to_all | solution.py:37
  21.3 4.4 all-to-all-done
  26.0 3.0 collective-permute-start
  30.6 4.4 collective-permute-done.1
  35.3 92.4 %while.24 = (s32[]{:T(128)}, f32[1024,256]{1,0:T(8,128)S(1)}, s32[27,1024]{1,0:T(8,128)}, bf16[1281,96]{1,0:T(8,128)(2,1)S(1)}, bf16[27,96,256]{2,1,0:T(8,128)(2,1)}, /*index=5*/s32[]{:T(128)}, s32[]{:T(128)}) while((s32[]{:T(128)}, f32[1024,256]{1,0:T(8,128)S(1)}, s32[27,1024]{1,0:T(8,128)}, bf16[1281,96]{1,0:T(8,128)(2,1)S(1)}, ...), condition=%wide.region_1.2_spmd.clone, body=%wide.region_0.1_spmd.clone.sunk | while | flops 304120832 | bytes 2404647 | solution.py:57
  36.2 2.6 convolution_add_fusion.4
  39.6 2.6 convolution_add_fusion.4
  43.0 2.6 convolution_add_fusion.4
  46.4 2.6 convolution_add_fusion.4
  49.8 2.6 convolution_add_fusion.4
  53.3 2.6 convolution_add_fusion.4
  56.7 2.6 convolution_add_fusion.4
  60.1 2.6 convolution_add_fusion.4
  63.5 2.6 convolution_add_fusion.4
  66.9 2.6 convolution_add_fusion.4
  70.4 2.6 convolution_add_fusion.4
  73.8 2.6 convolution_add_fusion.4
  77.2 2.6 convolution_add_fusion.4
  80.6 2.6 convolution_add_fusion.4
  84.0 2.6 convolution_add_fusion.4
  87.5 2.6 convolution_add_fusion.4
  90.9 2.6 convolution_add_fusion.4
  94.3 2.6 convolution_add_fusion.4
  97.7 2.6 convolution_add_fusion.4
  101.1 2.6 convolution_add_fusion.4
  104.5 2.6 convolution_add_fusion.4
  108.0 2.6 convolution_add_fusion.4
  111.4 2.6 convolution_add_fusion.4
  114.8 2.6 convolution_add_fusion.4
  118.2 2.6 convolution_add_fusion.4
  121.6 2.6 convolution_add_fusion.4
  125.1 2.6 convolution_add_fusion.4
  127.9 176.2 %while.25 = (s32[]{:T(128)}, f32[1281,96]{0,1:T(8,128)S(1)}, f32[27,96,256]{2,1,0:T(8,128)}, s32[27,1024]{1,0:T(8,128)}, bf16[27,96,256]{2,1,0:T(8,128)(2,1)}, /...) while((s32[]{:T(128)}, f32[1281,96]{0,1:T(8,128)S(1)}, ...), condition=%wide.region_3.4_spmd.clone, body=%wide.region_2.3_spmd.clone.sunk | while | flops 861121792 | bytes 4609851 | solution.py:79
  132.3 2.1 fusion.103
  138.9 2.1 fusion.103
  145.4 2.1 fusion.103
  151.9 2.1 fusion.103
  158.4 2.1 fusion.103
  165.0 2.1 fusion.103
  171.5 2.1 fusion.103
  178.0 2.1 fusion.103
  191.1 2.1 fusion.103
  304.2 59.4 %all-reduce.3.cloned.1.call-done = f32[27,96,256]{2,1,0:T(8,128)} async-done(((f32[27,96,256]{2,1,0:T(8,128)}), f32[27,96,256]{2,1,0:T(8,128)}) %all-reduce.3.cloned.1.call-update) | async-done | bytes 2654224 | tf_op jit(solution)/shard_map/psum | solution.py:80
  365.0 4.5 collective-permute-start.2
  372.7 7.2 %all-to-all-start.1 = ((bf16[8,128,96]{1,2,0:T(8,128)(2,1)}), bf16[8,128,96]{1,2,0:T(8,128)(2,1)S(1)}, u32[]{:S(2)}, u32[]{:S(2)}) async-start(bf16[8,128,96]{1,2,0:T(8,128)(2,1)} %bitcast.52), calls=%async_computation.1 | async-start | bytes 393216 | tf_op jit(solution)/shard_map/all_to_all | solution.py:92
  380.8 12.8 %all-to-all-done.1 = bf16[8,128,96]{1,2,0:T(8,128)(2,1)S(1)} async-done(((bf16[8,128,96]{1,2,0:T(8,128)(2,1)}), bf16[8,128,96]{1,2,0:T(8,128)(2,1)S(1)}, u32[]{:S(2)}, u32[]{:S(2)}) %all-to-all-start.1) | async-done | bytes 196640 | tf_op jit(solution)/shard_map/all_to_all | solution.py:92
  395.1 92.5 %all-reduce.5.cloned.1.call-done = f32[27,96,256]{2,1,0:T(8,128)} async-done(((f32[27,96,256]{2,1,0:T(8,128)}), f32[27,96,256]{2,1,0:T(8,128)}) %all-reduce.5.cloned.1.call-update) | async-done | bytes 2654224 | tf_op jit(solution)/shard_map/psum | solution.py:81
  487.6 3.6 broadcast_multiply_fusion
  (195 shorter events, 193.6 us)
Async XLA Ops:
  7.2 0.9 copy-start
  10.5 15.2 %all-to-all-start = ((bf16[8,128,96]{1,2,0:T(8,128)(2,1)}), bf16[8,128,96]{1,2,0:T(8,128)(2,1)S(1)}, u32[]{:S(2)}, u32[]{:S(2)}) async-start(bf16[8,128,96]{1,2,0:T(8,128)(2,1)} %bitcast.53), calls=%async_computation | async-start | bytes 393216 | tf_op jit(solution)/shard_map/all_to_all | solution.py:37
  17.8 345.9 %all-reduce.3.cloned.1.call-start = ((), (), s32[]{:S(2)}) async-start(), calls=%async_computation.2 | async-start | bytes 5308416 | tf_op jit(solution)/shard_map/psum | solution.py:80
  26.0 4.6 collective-permute-start
  29.3 5.7 %collective-permute-start.1 = (bf16[128,96]{0,1:T(8,128)(2,1)S(1)}, bf16[128,96]{0,1:T(8,128)(2,1)S(1)}, u32[]{:S(2)}, u32[]{:S(2)}) collective-permute-start(bf16[128,96]{0,1:T(8,128)(2,1)S(1)} %convolution_convert_fusion), channel_id=1, source_target_pairs={{4,0},{8,4},{12,8},{16,12},{20,16},{24,20},{28,24},{5,1},{9,5},{13... | collective-permute-start | bytes 73736 | tf_op jit(solution)/shard_map/ppermute | solution.py:11
  35.3 92.4 %copy-start.1 = (bf16[1024,256]{1,0:T(8,128)(2,1)S(1)}, bf16[1024,256]{1,0:T(8,128)(2,1)}, u32[]{:S(2)}) copy-start(bf16[1024,256]{1,0:T(8,128)(2,1)} %param.19) | copy-start | bytes 1572868
  35.3 92.4 %copy-start.2 = (f32[256]{0:T(256)S(1)}, f32[256]{0:T(256)}, u32[]{:S(2)}) copy-start(f32[256]{0:T(256)} %param.18) | copy-start | bytes 3076
  304.2 183.4 %all-reduce.5.cloned.1.call-start = ((), (), s32[]{:S(2)}) async-start(), calls=%async_computation.3 | async-start | bytes 5308416 | tf_op jit(solution)/shard_map/psum | solution.py:81
  363.7 5.9 %collective-permute-start.3 = (bf16[128,96]{0,1:T(8,128)(2,1)S(1)}, bf16[128,96]{0,1:T(8,128)(2,1)S(1)}, u32[]{:S(2)}, u32[]{:S(2)}) collective-permute-start(bf16[128,96]{0,1:T(8,128)(2,1)S(1)} %get-tuple-element.150), channel_id=1, source_target_pairs={{4,0},{8,4},{12,8},{16,12},{20,16},{24,20},{28,24},{5,1},{9,5},{13... | collective-permute-start | bytes 73736 | tf_op jit(solution)/shard_map/ppermute | solution.py:11
  365.0 6.1 %collective-permute-start.2 = (bf16[128,96]{0,1:T(8,128)(2,1)S(1)}, bf16[128,96]{0,1:T(8,128)(2,1)S(1)}, u32[]{:S(2)}, u32[]{:S(2)}) collective-permute-start(bf16[128,96]{0,1:T(8,128)(2,1)S(1)} %get-tuple-element.149), channel_id=1, source_target_pairs={{0,4},{4,8},{8,12},{12,16},{16,20},{20,24},{24,28},{1,5},{5,9},{9,... | collective-permute-start | bytes 73736 | tf_op jit(solution)/shard_map/ppermute | solution.py:11
  369.9 23.7 %copy-start.3 = (s32[1024]{0:T(1024)S(1)}, s32[1024]{0:T(1024)}, u32[]{:S(2)}) copy-start(s32[1024]{0:T(1024)} %param.13) | copy-start | bytes 12292
  372.7 20.9 %all-to-all-start.1 = ((bf16[8,128,96]{1,2,0:T(8,128)(2,1)}), bf16[8,128,96]{1,2,0:T(8,128)(2,1)S(1)}, u32[]{:S(2)}, u32[]{:S(2)}) async-start(bf16[8,128,96]{1,2,0:T(8,128)(2,1)} %bitcast.52), calls=%async_computation.1 | async-start | bytes 393216 | tf_op jit(solution)/shard_map/all_to_all | solution.py:92
Sparse Core Ops, SparseCore 0:
  304.3 59.3 all-reduce.2
  367.3 120.2 all-reduce.4
